TPU v7x, 32 devices: a whole 2x2x4 slice. The times are simulated.
32 devices in a mesh: rep: 8 (over y, x, core), shard: 4 (over z).
Axes of the slice: x: 2, y: 2, z: 4, core: 2. Of those that a mesh axis runs over, the one named last changes fastest.
Arguments:
- tokens: bfloat16 [16384, 1536], P(('rep', 'shard')), may hold values from -6 to 6
- cotangent: bfloat16 [16384, 1536], P(('rep', 'shard')), may hold values from -6 to 6
- norm_first: bfloat16 [1536], P('shard'), may hold values from 0.5 to 1.5
- branch_weight: bfloat16 [1536, 2048], P(None, 'shard'), may hold values from -0.15625 to 0.15625
- gelu_weight: bfloat16 [1536, 2048], P(None, 'shard'), may hold values from -0.15625 to 0.15625
- conv_weight: bfloat16 [4, 2048], P(None, 'shard'), may hold values from -2.5 to 2.5
- conv_bias: bfloat16 [2048], P('shard'), may hold values from -2.5 to 2.5
- gate_weight: bfloat16 [16, 128, 256], P('shard'), may hold values from -0.5 to 0.5
- gate_bias: bfloat16 [16, 256], P('shard'), may hold values from -2.5 to 2.5
- decay_param: bfloat16 [2048], P('shard'), may hold values from 2.1875 to 6.875
- merge_weight: bfloat16 [2048, 1536], P('shard'), may hold values from -0.375 to 0.375
- norm_second: bfloat16 [1536], P('shard'), may hold values from 0.5 to 1.5
- feed_gate: bfloat16 [1536, 4608], P(None, 'shard'), may hold values from -0.15625 to 0.15625
- feed_up: bfloat16 [1536, 4608], P(None, 'shard'), may hold values from -0.15625 to 0.15625
- feed_down: bfloat16 [4608, 1536], P('shard'), may hold values from -0.1875 to 0.1875
- down_branch: bfloat16 [1536, 128], P(None, 'shard'), may hold values from -0.15625 to 0.15625
- up_branch: bfloat16 [128, 2048], P('shard'), may hold values from -0.75 to 0.75
- down_gelu: bfloat16 [1536, 128], P(None, 'shard'), may hold values from -0.15625 to 0.15625
- up_gelu: bfloat16 [128, 2048], P('shard'), may hold values from -0.75 to 0.75
- down_gates: bfloat16 [2048, 128], P(None, 'shard'), may hold values from -0.125 to 0.125
- up_gates: bfloat16 [128, 4096], P('shard'), may hold values from -0.75 to 0.75
- down_merge: bfloat16 [2048, 128], P(None, 'shard'), may hold values from -0.125 to 0.125
- up_merge: bfloat16 [128, 1536], P('shard'), may hold values from -0.75 to 0.75
- down_feed_gate: bfloat16 [1536, 128], P(None, 'shard'), may hold values from -0.15625 to 0.15625
- up_feed_gate: bfloat16 [128, 4608], P('shard'), may hold values from -0.75 to 0.75
- down_feed_up: bfloat16 [1536, 128], P(None, 'shard'), may hold values from -0.15625 to 0.15625
- up_feed_up: bfloat16 [128, 4608], P('shard'), may hold values from -0.75 to 0.75
- down_feed_down: bfloat16 [4608, 128], P(None, 'shard'), may hold values from -0.09375 to 0.09375
- up_feed_down: bfloat16 [128, 1536], P('shard'), may hold values from -0.75 to 0.75
- seq_lengths: int32 [32, 4], P(('rep', 'shard')), may hold values from 1 to 256, 384 in all within a row
- adapter_index: int32 [32, 4], P(('rep', 'shard')), may hold values from 0 to 7
- deal_order: int32 [8, 2048], P('rep'), may hold values from 0 to 2047, as said below
Outputs:
- layer_out: float32 [16384, 1536], P(('rep', 'shard'))
- grad_tokens: float32 [16384, 1536], P(('rep', 'shard'))
- grad_down_branch: float32 [1536, 128], P(None, 'shard')
- grad_up_branch: float32 [128, 2048], P('shard')
- grad_down_gelu: float32 [1536, 128], P(None, 'shard')
- grad_up_gelu: float32 [128, 2048], P('shard')
- grad_down_gates: float32 [2048, 128], P(None, 'shard')
- grad_up_gates: float32 [128, 4096], P('shard')
- grad_down_merge: float32 [2048, 128], P(None, 'shard')
- grad_up_merge: float32 [128, 1536], P('shard')
- grad_down_feed_gate: float32 [1536, 128], P(None, 'shard')
- grad_up_feed_gate: float32 [128, 4608], P('shard')
- grad_down_feed_up: float32 [1536, 128], P(None, 'shard')
- grad_up_feed_up: float32 [128, 4608], P('shard')
- grad_down_feed_down: float32 [4608, 128], P(None, 'shard')
- grad_up_feed_down: float32 [128, 1536], P('shard')
Inputs may be any that keep to these rules, and one draw needn't show every extreme that they name: Each row of deal_order is a permutation of 0 to 2047. Exactly 128 of the arrival rows of one device (rows b * 512 to b * 512 + 511 of its group) fill slots of each block of its group. `seq_lengths`: in every block the lengths sum to 384 and the longest is 256.
All inputs are finite; a program needn't handle non-finite values.
Results may differ from a plain program's by a relative error of at most 0.015.
Values may be sent and summed in bfloat16 or wider, within the bound.
A program may use at most 320 MiB of HBM per device.

v0:
```python
import jax
import jax.numpy as jnp
from jax import lax
from jax.sharding import PartitionSpec as P

H = 16
DH = 128
NA = 8
R = 16
NORM_EPSILON = 1e-06
DECAY_SCALE = 8.0


def matmul(left, right):
    return jnp.dot(left, right, preferred_element_type=jnp.float32)


def matmul_right_t(left, right):
    return lax.dot_general(
        left, right, (((1,), (1,)), ((), ())), preferred_element_type=jnp.float32
    )


def matmul_left_t(left, right):
    return lax.dot_general(
        left, right, (((0,), (0,)), ((), ())), preferred_element_type=jnp.float32
    )


def root_norm(values, gain):
    return (
        values * lax.rsqrt(jnp.mean(values * values, axis=-1, keepdims=True) + NORM_EPSILON) * gain
    )


def layout(lengths_row, index_row, slots_count):
    seq_count = lengths_row.shape[0]
    ends = jnp.cumsum(lengths_row)
    starts = ends - lengths_row
    slots = jnp.arange(slots_count, dtype=jnp.int32)
    segment = jnp.sum((slots[:, None] >= ends[None, :]).astype(jnp.int32), axis=1)
    start_all = jnp.concatenate([starts, ends[-1:]])
    member = segment[:, None] == jnp.arange(seq_count + 1, dtype=jnp.int32)[None, :]
    position = slots - jnp.sum(jnp.where(member, start_all[None, :], 0), axis=1)
    live_rows = segment < seq_count
    chosen = jnp.sum(jnp.where(member[:, :seq_count], index_row[None, :], 0), axis=1)
    adapter_hit = (chosen[:, None] == jnp.arange(NA, dtype=jnp.int32)[None, :]) & live_rows[:, None]
    adapter_mask = jnp.repeat(adapter_hit.astype(jnp.float32), R, axis=1)
    return (position, live_rows.astype(jnp.float32), adapter_mask)


def conv_apply(values, weight, bias, position):
    total = bias[None, :] + weight[0][None, :] * values
    for offset in range(1, weight.shape[0]):
        moved = jnp.concatenate(
            [jnp.zeros((offset, values.shape[1]), values.dtype), values[:-offset]], axis=0
        )
        keeper = (position >= offset).astype(values.dtype)[:, None]
        total = total + weight[offset][None, :] * moved * keeper
    return total


def combine(earlier, later):
    return (earlier[0] * later[0], later[0] * earlier[1] + later[1])


def recurrence(gate_logits, conv_out, gelu_in, decay, position):
    rows_count = conv_out.shape[0]
    shaped = gate_logits.reshape(rows_count, H, 2 * DH)
    input_gate = jax.nn.sigmoid(shaped[:, :, :DH]).reshape(rows_count, H * DH)
    rec_gate = jax.nn.sigmoid(shaped[:, :, DH:]).reshape(rows_count, H * DH)
    log_decay = -DECAY_SCALE * rec_gate * jax.nn.softplus(-decay)[None, :]
    decay_now = jnp.exp(log_decay)
    first = (position == 0)[:, None]
    scale_in = jnp.where(first, 1.0, jnp.sqrt(-jnp.expm1(2.0 * log_decay)))
    carried = jnp.where(first, 0.0, decay_now)
    driven = scale_in * input_gate * conv_out
    unused, state = lax.associative_scan(combine, (carried, driven), axis=0)
    return state * jax.nn.gelu(gelu_in)


def feed_mix(hidden_gate, hidden_up):
    return jax.nn.gelu(hidden_gate) * hidden_up


def local(
    tokens,
    cotangent,
    norm_first,
    branch_weight,
    gelu_weight,
    conv_weight,
    conv_bias,
    gate_weight,
    gate_bias,
    decay_param,
    merge_weight,
    norm_second,
    feed_gate,
    feed_up,
    feed_down,
    down_branch,
    up_branch,
    down_gelu,
    up_gelu,
    down_gates,
    up_gates,
    down_merge,
    up_merge,
    down_feed_gate,
    up_feed_gate,
    down_feed_up,
    up_feed_up,
    down_feed_down,
    up_feed_down,
    seq_lengths,
    adapter_index,
    deal_order,
):
    rows_here = tokens.shape[0]
    shards = lax.axis_size("shard")
    my_index = lax.axis_index("shard")
    deal_row = deal_order[0]
    group_rows = deal_row.shape[0]
    gathered = (
        lax.all_gather(tokens, "shard", axis=0, tiled=True),
        lax.all_gather(cotangent, "shard", axis=0, tiled=True),
    )
    my_picks = lax.dynamic_slice_in_dim(deal_row, my_index * rows_here, rows_here)
    work_in = jnp.take(gathered[0], my_picks, axis=0)
    work_cot = jnp.take(gathered[1], my_picks, axis=0)
    block_parts = (
        lax.all_gather(norm_first, "shard", axis=0, tiled=True),
        lax.all_gather(branch_weight, "shard", axis=1, tiled=True),
        lax.all_gather(gelu_weight, "shard", axis=1, tiled=True),
        lax.all_gather(conv_weight, "shard", axis=1, tiled=True),
        lax.all_gather(conv_bias, "shard", axis=0, tiled=True),
        lax.all_gather(gate_weight, "shard", axis=0, tiled=True),
        lax.all_gather(gate_bias, "shard", axis=0, tiled=True),
        lax.all_gather(decay_param, "shard", axis=0, tiled=True),
        lax.all_gather(merge_weight, "shard", axis=0, tiled=True),
    )
    (
        gain_first,
        weight_branch,
        weight_gelu,
        taps_conv,
        bias_conv,
        weight_gates,
        bias_gates,
        decay_all,
        weight_merge,
    ) = block_parts
    adapter_parts = (
        lax.all_gather(down_branch, "shard", axis=1, tiled=True),
        lax.all_gather(up_branch, "shard", axis=0, tiled=True),
        lax.all_gather(down_gelu, "shard", axis=1, tiled=True),
        lax.all_gather(up_gelu, "shard", axis=0, tiled=True),
        lax.all_gather(down_gates, "shard", axis=1, tiled=True),
        lax.all_gather(up_gates, "shard", axis=0, tiled=True),
        lax.all_gather(down_merge, "shard", axis=1, tiled=True),
        lax.all_gather(up_merge, "shard", axis=0, tiled=True),
        lax.all_gather(down_feed_gate, "shard", axis=1, tiled=True),
        lax.all_gather(up_feed_gate, "shard", axis=0, tiled=True),
        lax.all_gather(down_feed_up, "shard", axis=1, tiled=True),
        lax.all_gather(up_feed_up, "shard", axis=0, tiled=True),
        lax.all_gather(down_feed_down, "shard", axis=1, tiled=True),
        lax.all_gather(up_feed_down, "shard", axis=0, tiled=True),
    )
    (
        fact_down_branch,
        fact_up_branch,
        fact_down_gelu,
        fact_up_gelu,
        fact_down_gates,
        fact_up_gates,
        fact_down_merge,
        fact_up_merge,
        fact_down_fgate,
        fact_up_fgate,
        fact_down_fup,
        fact_up_fup,
        fact_down_fdown,
        fact_up_fdown,
    ) = adapter_parts
    position, live_rows, adapter_mask = layout(seq_lengths[0], adapter_index[0], rows_here)

    def adapter_forward(act, down, up):
        rank_part = (matmul(act, down) * adapter_mask).astype(jnp.bfloat16)
        return (rank_part, matmul(rank_part, up))

    def adapter_backward(grad_low, act, rank_part, up):
        grad_rank = (matmul_right_t(grad_low, up) * adapter_mask).astype(jnp.bfloat16)
        return (grad_rank, matmul_left_t(act, grad_rank), matmul_left_t(rank_part, grad_low))

    gain_first_f = gain_first.astype(jnp.float32)
    rows_in = work_in.astype(jnp.float32)
    normed_first, first_pull = jax.vjp(lambda values: root_norm(values, gain_first_f), rows_in)
    act_first = normed_first.astype(jnp.bfloat16)
    rank_branch, extra_branch = adapter_forward(act_first, fact_down_branch, fact_up_branch)
    branch = matmul(act_first, weight_branch) + extra_branch
    rank_gelu, extra_gelu = adapter_forward(act_first, fact_down_gelu, fact_up_gelu)
    gelu_in = matmul(act_first, weight_gelu) + extra_gelu
    taps_f = taps_conv.astype(jnp.float32)
    bias_f = bias_conv.astype(jnp.float32)
    conv_out, conv_pull = jax.vjp(
        lambda values: conv_apply(values, taps_f, bias_f, position), branch
    )
    conv_low = conv_out.astype(jnp.bfloat16)
    heads = conv_low.reshape(rows_here, H, DH)
    blockwise = jnp.einsum(
        "thd,hde->the", heads, weight_gates, preferred_element_type=jnp.float32
    ).reshape(rows_here, 2 * H * DH)
    rank_gates, extra_gates = adapter_forward(conv_low, fact_down_gates, fact_up_gates)
    gate_logits = blockwise + bias_gates.astype(jnp.float32).reshape(-1)[None, :] + extra_gates
    decay_f = decay_all.astype(jnp.float32)
    mixed, mixed_pull = jax.vjp(
        lambda logits, conv_in, gelu_part: recurrence(
            logits, conv_in, gelu_part, decay_f, position
        ),
        gate_logits,
        conv_out,
        gelu_in,
    )
    mixed_low = mixed.astype(jnp.bfloat16)
    rank_merge, extra_merge = adapter_forward(mixed_low, fact_down_merge, fact_up_merge)
    resid = rows_in + matmul(mixed_low, weight_merge) + extra_merge
    feed_parts = (
        lax.all_gather(norm_second, "shard", axis=0, tiled=True),
        lax.all_gather(feed_gate, "shard", axis=1, tiled=True),
        lax.all_gather(feed_up, "shard", axis=1, tiled=True),
        lax.all_gather(feed_down, "shard", axis=0, tiled=True),
    )
    gain_second, weight_fgate, weight_fup, weight_fdown = feed_parts
    gain_second_f = gain_second.astype(jnp.float32)
    normed_second, second_pull = jax.vjp(lambda values: root_norm(values, gain_second_f), resid)
    act_second = normed_second.astype(jnp.bfloat16)
    rank_fgate, extra_fgate = adapter_forward(act_second, fact_down_fgate, fact_up_fgate)
    hidden_gate = matmul(act_second, weight_fgate) + extra_fgate
    rank_fup, extra_fup = adapter_forward(act_second, fact_down_fup, fact_up_fup)
    hidden_up = matmul(act_second, weight_fup) + extra_fup
    hidden, hidden_pull = jax.vjp(feed_mix, hidden_gate, hidden_up)
    hidden_low = hidden.astype(jnp.bfloat16)
    rank_fdown, extra_fdown = adapter_forward(hidden_low, fact_down_fdown, fact_up_fdown)
    work_out = (resid + matmul(hidden_low, weight_fdown) + extra_fdown) * live_rows[:, None]
    grad_out = work_cot.astype(jnp.float32) * live_rows[:, None]
    grad_out_low = grad_out.astype(jnp.bfloat16)
    grad_rank_fdown, grad_down_fdown, grad_up_fdown = adapter_backward(
        grad_out_low, hidden_low, rank_fdown, fact_up_fdown
    )
    grad_hidden = matmul_right_t(grad_out_low, weight_fdown) + matmul_right_t(
        grad_rank_fdown, fact_down_fdown
    )
    grad_hgate, grad_hup = hidden_pull(grad_hidden)
    grad_hgate_low = grad_hgate.astype(jnp.bfloat16)
    grad_hup_low = grad_hup.astype(jnp.bfloat16)
    grad_rank_fgate, grad_down_fgate, grad_up_fgate = adapter_backward(
        grad_hgate_low, act_second, rank_fgate, fact_up_fgate
    )
    grad_rank_fup, grad_down_fup, grad_up_fup = adapter_backward(
        grad_hup_low, act_second, rank_fup, fact_up_fup
    )
    grad_second = (
        matmul_right_t(grad_hgate_low, weight_fgate)
        + matmul_right_t(grad_hup_low, weight_fup)
        + matmul_right_t(grad_rank_fgate, fact_down_fgate)
        + matmul_right_t(grad_rank_fup, fact_down_fup)
    )
    grad_resid = grad_out + second_pull(grad_second)[0]
    grad_resid_low = grad_resid.astype(jnp.bfloat16)
    grad_rank_merge, grad_down_merge, grad_up_merge = adapter_backward(
        grad_resid_low, mixed_low, rank_merge, fact_up_merge
    )
    grad_mixed = matmul_right_t(grad_resid_low, weight_merge) + matmul_right_t(
        grad_rank_merge, fact_down_merge
    )
    grad_logits, grad_conv_direct, grad_gelu_in = mixed_pull(grad_mixed)
    grad_logits_low = grad_logits.astype(jnp.bfloat16)
    grad_rank_gates, grad_down_gates, grad_up_gates = adapter_backward(
        grad_logits_low, conv_low, rank_gates, fact_up_gates
    )
    grad_heads = jnp.einsum(
        "the,hde->thd",
        grad_logits_low.reshape(rows_here, H, 2 * DH),
        weight_gates,
        preferred_element_type=jnp.float32,
    ).reshape(rows_here, H * DH)
    grad_conv = grad_conv_direct + grad_heads + matmul_right_t(grad_rank_gates, fact_down_gates)
    grad_branch = conv_pull(grad_conv)[0]
    grad_branch_low = grad_branch.astype(jnp.bfloat16)
    grad_gelu_low = grad_gelu_in.astype(jnp.bfloat16)
    grad_rank_branch, grad_down_branch, grad_up_branch = adapter_backward(
        grad_branch_low, act_first, rank_branch, fact_up_branch
    )
    grad_rank_gelu, grad_down_gelu, grad_up_gelu = adapter_backward(
        grad_gelu_low, act_first, rank_gelu, fact_up_gelu
    )
    grad_first = (
        matmul_right_t(grad_branch_low, weight_branch)
        + matmul_right_t(grad_gelu_low, weight_gelu)
        + matmul_right_t(grad_rank_branch, fact_down_branch)
        + matmul_right_t(grad_rank_gelu, fact_down_gelu)
    )
    grad_work = grad_resid + first_pull(grad_first)[0]
    collected = (
        lax.all_gather(work_out, "shard", axis=0, tiled=True),
        lax.all_gather(grad_work, "shard", axis=0, tiled=True),
    )
    inverse = (
        jnp.zeros((group_rows,), jnp.int32)
        .at[deal_row]
        .set(jnp.arange(group_rows, dtype=jnp.int32))
    )
    my_rows = lax.dynamic_slice_in_dim(inverse, my_index * rows_here, rows_here)
    layer_out = jnp.take(collected[0], my_rows, axis=0)
    grad_tokens = jnp.take(collected[1], my_rows, axis=0)
    part_width = grad_down_branch.shape[1] // shards
    summed = lax.psum(
        (
            grad_down_branch,
            grad_up_branch,
            grad_down_gelu,
            grad_up_gelu,
            grad_down_gates,
            grad_up_gates,
            grad_down_merge,
            grad_up_merge,
            grad_down_fgate,
            grad_up_fgate,
            grad_down_fup,
            grad_up_fup,
            grad_down_fdown,
            grad_up_fdown,
        ),
        ("rep", "shard"),
    )
    owned = tuple(
        (
            lax.dynamic_slice_in_dim(
                summed[number], my_index * part_width, part_width, 1 - number % 2
            )
            for number in range(14)
        )
    )
    return (
        layer_out,
        grad_tokens,
        owned[0],
        owned[1],
        owned[2],
        owned[3],
        owned[4],
        owned[5],
        owned[6],
        owned[7],
        owned[8],
        owned[9],
        owned[10],
        owned[11],
        owned[12],
        owned[13],
    )


def solution(mesh):
    in_specs = (
        P(("rep", "shard"), None),
        P(("rep", "shard"), None),
        P("shard"),
        P(None, "shard"),
        P(None, "shard"),
        P(None, "shard"),
        P("shard"),
        P("shard", None, None),
        P("shard", None),
        P("shard"),
        P("shard", None),
        P("shard"),
        P(None, "shard"),
        P(None, "shard"),
        P("shard", None),
        P(None, "shard"),
        P("shard", None),
        P(None, "shard"),
        P("shard", None),
        P(None, "shard"),
        P("shard", None),
        P(None, "shard"),
        P("shard", None),
        P(None, "shard"),
        P("shard", None),
        P(None, "shard"),
        P("shard", None),
        P(None, "shard"),
        P("shard", None),
        P(("rep", "shard"), None),
        P(("rep", "shard"), None),
        P("rep", None),
    )
    out_specs = (
        P(("rep", "shard"), None),
        P(("rep", "shard"), None),
        P(None, "shard"),
        P("shard", None),
        P(None, "shard"),
        P("shard", None),
        P(None, "shard"),
        P("shard", None),
        P(None, "shard"),
        P("shard", None),
        P(None, "shard"),
        P("shard", None),
        P(None, "shard"),
        P("shard", None),
        P(None, "shard"),
        P("shard", None),
    )
    return jax.shard_map(local, mesh=mesh, in_specs=in_specs, out_specs=out_specs, check_vma=False)
```

profile of v0, /device:TPU:0, one launch (start us, length us, event | category | flops | bytes accessed | tf_op | source)
XLA Modules:
  0.0 3010.1 jit_solution(17063541124897532782)
XLA Ops:
  19.0 15.6 all-gather.1
  35.0 17.7 all_gather.98
  52.7 23.4 all_gather.99
  76.9 16.7 all_gather.95
  93.6 14.6 all-gather
  108.3 20.1 all_gather.102
  128.4 15.4 all-gather.2
  143.8 12.0 all-gather.3
  156.5 17.4 all_gather.106
  173.8 23.5 all_gather.107
  197.3 24.9 all_gather.109
  222.2 22.7 all_gather.110
  244.9 12.1 all-gather.4
  257.6 20.9 all_gather.116
  278.5 22.2 all_gather.113
  300.7 15.2 all_gather.120
  347.6 8.9 copy.113
  362.9 8.3 add_add_fusion
  371.1 9.3 copy.142
  398.1 11.7 exponential_select_fusion
  409.8 9.8 slice.325
  419.6 9.8 slice.326
  429.5 9.8 slice.324
  439.3 9.8 slice.328
  556.3 10.1 slice.323
  566.5 10.1 slice.388
  598.7 8.7 pad.364
  616.3 16.5 pad.367
  638.7 16.5 pad.366
  678.3 31.0 %all-gather.47.cloned.1.call-done = bf16[2048,1536]{1,0:T(8,128)(2,1)} async-done(((bf16[512,1536]{1,0:T(8,128)(2,1)}), bf16[2048,1536]{1,0:T(8,128)(2,1)}) %all-gather.47.cloned.1.call-update) | async-done | bytes 6291472 | tf_op jit(solution)/shard_map/all_gather | solution.py:127
  709.3 8.2 gather_fusion.2
  720.0 233.1 %all-gather.37.cloned.1.call-done = bf16[1536,4608]{1,0:T(8,128)(2,1)} async-done(((bf16[1536,1152]{1,0:T(8,128)(2,1)}), bf16[1536,4608]{1,0:T(8,128)(2,1)}) %all-gather.37.cloned.1.call-update) | async-done | bytes 14155792 | tf_op jit(solution)/shard_map/all_gather | solution.py:231
  953.1 12.9 fusion.130
  965.9 230.9 %all-gather.33.cloned.1.call-done = bf16[1536,4608]{1,0:T(8,128)(2,1)} async-done(((bf16[1536,1152]{1,0:T(8,128)(2,1)}), bf16[1536,4608]{1,0:T(8,128)(2,1)}) %all-gather.33.cloned.1.call-update) | async-done | bytes 14155792 | tf_op jit(solution)/shard_map/all_gather | solution.py:230
  1196.8 12.8 fusion.129
  1209.7 17.2 all-gather.39.cloned.1.call-done
  1226.9 9.0 convolution_add_fusion.1
  1235.9 22.2 all-gather.35.cloned.1.call-done
  1258.1 10.0 convolution_add_fusion.2
  1268.1 234.5 %all-gather.41.cloned.1.call-done = bf16[4608,1536]{1,0:T(8,128)(2,1)} async-done(((bf16[1152,1536]{1,0:T(8,128)(2,1)}), bf16[4608,1536]{1,0:T(8,128)(2,1)}) %all-gather.41.cloned.1.call-update) | async-done | bytes 14155792 | tf_op jit(solution)/shard_map/all_gather | solution.py:232
  1502.6 13.4 fusion.95
  1516.0 16.8 all-gather.43.cloned.1.call-done
  1532.8 17.3 multiply_convert_fusion
  1550.1 13.4 fusion.131
  1564.9 10.3 convolution_add_fusion.12
  1598.4 9.8 slice.389
  1615.1 9.8 slice.390
  1714.0 8.8 pad.425
  1727.5 8.6 pad.450
  1736.2 8.7 pad.375
  1749.8 11.2 multiply_add_fusion.1
  1763.9 16.6 pad.426
  1780.5 16.5 pad.427
  1797.0 16.6 pad.451
  1813.6 16.6 pad.452
  1830.2 16.9 pad.370
  1847.1 16.9 pad.428
  1864.0 18.5 multiply_multiply_fusion.5
  1977.3 12.4 convolution_add_fusion.13
  2019.8 528.0 %all-reduce.96.cloned.1.call-done = (f32[1536,128]{0,1:T(8,128)}, f32[128,2048]{1,0:T(8,128)}, f32[1536,128]{0,1:T(8,128)}, f32[128,2048]{1,0:T(8,128)}, f32[204...) async-done(((f32[1536,128]{0,1:T(8,128)}, ...) | async-done | bytes 18087952 | tf_op jit(solution)/shard_map/psum | solution.py:318
  2563.3 207.1 %all-gather.45.cloned.1.call-done = f32[2048,1536]{1,0:T(8,128)} async-done(((f32[512,1536]{1,0:T(8,128)}), f32[2048,1536]{1,0:T(8,128)}) %all-gather.45.cloned.1.call-update) | async-done | bytes 12582928 | tf_op jit(solution)/shard_map/all_gather | solution.py:306
  2770.3 8.3 gather_fusion.1
  2778.6 210.2 %all-gather.49.cloned.1.call-done = f32[2048,1536]{1,0:T(8,128)} async-done(((f32[512,1536]{1,0:T(8,128)}), f32[2048,1536]{1,0:T(8,128)}) %all-gather.49.cloned.1.call-update) | async-done | bytes 12582928 | tf_op jit(solution)/shard_map/all_gather | solution.py:307
  2988.8 9.1 gather_fusion.3
  (797 shorter events, 515.4 us)
Async XLA Ops:
  7.2 310.7 %all-gather.21.cloned.1.call-start = ((), (), s32[]{:S(2)}) async-start(), calls=%async_computation | async-start | bytes 7864320 | tf_op jit(solution)/shard_map/all_gather | solution.py:126
  7.9 321.1 %all-gather.23.cloned.1.call-start = ((), (), s32[]{:S(2)}) async-start(), calls=%async_computation.1 | async-start | bytes 7864320 | tf_op jit(solution)/shard_map/all_gather | solution.py:134
  8.7 332.4 %all-gather.25.cloned.1.call-start = ((), (), s32[]{:S(2)}) async-start(), calls=%async_computation.2 | async-start | bytes 1310720 | tf_op jit(solution)/shard_map/all_gather | solution.py:138
  9.4 353.5 %all-gather.27.cloned.1.call-start = ((), (), s32[]{:S(2)}) async-start(), calls=%async_computation.3 | async-start | bytes 1310720 | tf_op jit(solution)/shard_map/all_gather | solution.py:160
  10.0 645.9 %all-gather.29.cloned.1.call-start = ((), (), s32[]{:S(2)}) async-start(), calls=%async_computation.4 | async-start | bytes 7864320 | tf_op jit(solution)/shard_map/all_gather | solution.py:135
  10.6 657.5 %all-gather.31.cloned.1.call-start = ((), (), s32[]{:S(2)}) async-start(), calls=%async_computation.5 | async-start | bytes 7864320 | tf_op jit(solution)/shard_map/all_gather | solution.py:141
  11.1 698.2 %all-gather.47.cloned.1.call-start = ((), (), s32[]{:S(2)}) async-start(), calls=%async_computation.13 | async-start | bytes 7864320 | tf_op jit(solution)/shard_map/all_gather | solution.py:127
  11.9 941.2 %all-gather.37.cloned.1.call-start = ((), (), s32[]{:S(2)}) async-start(), calls=%async_computation.8 | async-start | bytes 17694720 | tf_op jit(solution)/shard_map/all_gather | solution.py:231
  12.7 22.1 copy-start.211
  12.7 22.3 copy-start.168
  12.7 40.0 %copy-start.157 = (bf16[32,2048]{1,0:T(8,128)(2,1)S(1)}, bf16[32,2048]{1,0:T(8,128)(2,1)}, u32[]{:S(2)}) copy-start(bf16[32,2048]{1,0:T(8,128)(2,1)} %param.52) | copy-start | bytes 393220
  12.7 64.2 %copy-start.204 = (bf16[4,512]{1,0:T(4,128)(2,1)S(1)}, bf16[4,512]{1,0:T(4,128)(2,1)}, u32[]{:S(2)}) copy-start(bf16[4,512]{1,0:T(4,128)(2,1)} %param.41) | copy-start | bytes 12292
  12.7 80.9 %copy-start.206 = (bf16[512]{0:T(512)(128)(2,1)S(1)}, bf16[512]{0:T(512)(128)(2,1)}, u32[]{:S(2)}) copy-start(bf16[512]{0:T(512)(128)(2,1)} %param.42) | copy-start | bytes 3076
  12.7 1184.1 %all-gather.33.cloned.1.call-start = ((), (), s32[]{:S(2)}) async-start(), calls=%async_computation.6 | async-start | bytes 17694720 | tf_op jit(solution)/shard_map/all_gather | solution.py:230
  13.4 94.8 %copy-start.158 = (bf16[2048,32]{0,1:T(8,128)(2,1)S(1)}, bf16[2048,32]{0,1:T(8,128)(2,1)}, u32[]{:S(2)}) copy-start(bf16[2048,32]{0,1:T(8,128)(2,1)} %param.55) | copy-start | bytes 393220
  13.5 114.9 %copy-start.205 = (bf16[4,256]{1,0:T(4,128)(2,1)S(1)}, bf16[4,256]{1,0:T(4,128)(2,1)}, u32[]{:S(2)}) copy-start(bf16[4,256]{1,0:T(4,128)(2,1)} %param.44) | copy-start | bytes 6148
  13.5 130.4 %copy-start.207 = (bf16[512]{0:T(512)(128)(2,1)S(1)}, bf16[512]{0:T(512)(128)(2,1)}, u32[]{:S(2)}) copy-start(bf16[512]{0:T(512)(128)(2,1)} %param.45) | copy-start | bytes 3076
  13.5 143.0 %copy-start.169 = (bf16[1536,32]{0,1:T(8,128)(2,1)S(1)}, bf16[1536,32]{0,1:T(8,128)(2,1)}, u32[]{:S(2)}) copy-start(bf16[1536,32]{0,1:T(8,128)(2,1)} %param.53) | copy-start | bytes 294916
  13.5 160.3 %copy-start.159 = (bf16[32,2048]{1,0:T(8,128)(2,1)S(1)}, bf16[32,2048]{1,0:T(8,128)(2,1)}, u32[]{:S(2)}) copy-start(bf16[32,2048]{1,0:T(8,128)(2,1)} %param.54) | copy-start | bytes 393220
  13.5 1213.4 %all-gather.39.cloned.1.call-start = ((), (), s32[]{:S(2)}) async-start(), calls=%async_computation.9 | async-start | bytes 1474560 | tf_op jit(solution)/shard_map/all_gather | solution.py:166
  14.1 183.2 %copy-start.160 = (bf16[2048,32]{0,1:T(8,128)(2,1)S(1)}, bf16[2048,32]{0,1:T(8,128)(2,1)}, u32[]{:S(2)}) copy-start(bf16[2048,32]{0,1:T(8,128)(2,1)} %param.57) | copy-start | bytes 393220
  14.1 1244.0 %all-gather.35.cloned.1.call-start = ((), (), s32[]{:S(2)}) async-start(), calls=%async_computation.7 | async-start | bytes 1474560 | tf_op jit(solution)/shard_map/all_gather | solution.py:164
  14.8 207.3 %copy-start.170 = (bf16[32,1536]{1,0:T(8,128)(2,1)S(1)}, bf16[32,1536]{1,0:T(8,128)(2,1)}, u32[]{:S(2)}) copy-start(bf16[32,1536]{1,0:T(8,128)(2,1)} %param.58) | copy-start | bytes 294916
  14.8 230.0 %copy-start.209 = (bf16[384]{0:T(512)(128)(2,1)S(1)}, bf16[384]{0:T(512)(128)(2,1)}, u32[]{:S(2)}) copy-start(bf16[384]{0:T(512)(128)(2,1)} %param.47) | copy-start | bytes 2308
  14.9 242.7 %copy-start.171 = (bf16[1536,32]{0,1:T(8,128)(2,1)S(1)}, bf16[1536,32]{0,1:T(8,128)(2,1)}, u32[]{:S(2)}) copy-start(bf16[1536,32]{0,1:T(8,128)(2,1)} %param.61) | copy-start | bytes 294916
  14.9 263.6 %copy-start.172 = (bf16[1536,32]{0,1:T(8,128)(2,1)S(1)}, bf16[1536,32]{0,1:T(8,128)(2,1)}, u32[]{:S(2)}) copy-start(bf16[1536,32]{0,1:T(8,128)(2,1)} %param.59) | copy-start | bytes 294916
  14.9 285.8 %copy-start.173 = (bf16[32,1536]{1,0:T(8,128)(2,1)S(1)}, bf16[32,1536]{1,0:T(8,128)(2,1)}, u32[]{:S(2)}) copy-start(bf16[32,1536]{1,0:T(8,128)(2,1)} %param.64) | copy-start | bytes 294916
  14.9 1487.7 %all-gather.41.cloned.1.call-start = ((), (), s32[]{:S(2)}) async-start(), calls=%async_computation.10 | async-start | bytes 17694720 | tf_op jit(solution)/shard_map/all_gather | solution.py:232
  15.5 1517.3 %all-gather.43.cloned.1.call-start = ((), (), s32[]{:S(2)}) async-start(), calls=%async_computation.11 | async-start | bytes 1474560 | tf_op jit(solution)/shard_map/all_gather | solution.py:167
  16.2 2531.6 %all-reduce.96.cloned.1.call-start = ((), (), s32[]{:S(2)}) async-start(), calls=%async_computation.15 | async-start | bytes 36175872 | tf_op jit(solution)/shard_map/psum | solution.py:318
  34.7 291.6 %copy-start.177 = (f32[1536]{0:T(1024)}, f32[1536]{0:T(1024)S(1)}, u32[]{:S(2)}) copy-start(f32[1536]{0:T(1024)S(1)} %reshape.246) | copy-start | bytes 18436
  52.7 275.7 %copy-start.72 = (bf16[1536,128]{0,1:T(8,128)(2,1)}, bf16[1536,128]{0,1:T(8,128)(2,1)S(1)}, u32[]{:S(2)}) copy-start(bf16[1536,128]{0,1:T(8,128)(2,1)S(1)} %all_gather.98) | copy-start | bytes 1179652
  76.0 258.5 %copy-start.49 = (bf16[128,2048]{1,0:T(8,128)(2,1)}, bf16[128,2048]{1,0:T(8,128)(2,1)S(1)}, u32[]{:S(2)}) copy-start(bf16[128,2048]{1,0:T(8,128)(2,1)S(1)} %all_gather.99) | copy-start | bytes 1572868
  76.8 321.3 %copy-start.198 = (pred[512]{0:T(512)(128)(4,1)}, pred[512]{0:T(512)(128)(4,1)S(1)}, u32[]{:S(2)}) copy-start(pred[512]{0:T(512)(128)(4,1)S(1)} %get-tuple-element.146) | copy-start | bytes 1540
  93.6 241.7 %copy-start.175 = (f32[1,2048]{1,0:T(1,128)}, f32[1,2048]{1,0:T(1,128)S(1)}, u32[]{:S(2)}) copy-start(f32[1,2048]{1,0:T(1,128)S(1)} %get-tuple-element.140) | copy-start | bytes 24580
  93.6 241.7 %copy-start.179 = (f32[1,2048]{1,0:T(1,128)}, f32[1,2048]{1,0:T(1,128)S(1)}, u32[]{:S(2)}) copy-start(f32[1,2048]{1,0:T(1,128)S(1)} %get-tuple-element.141) | copy-start | bytes 24580
  93.6 241.7 %copy-start.181 = (f32[1,2048]{1,0:T(1,128)}, f32[1,2048]{1,0:T(1,128)S(1)}, u32[]{:S(2)}) copy-start(f32[1,2048]{1,0:T(1,128)S(1)} %get-tuple-element.143) | copy-start | bytes 24580
  93.6 241.7 %copy-start.183 = (f32[1,2048]{1,0:T(1,128)}, f32[1,2048]{1,0:T(1,128)S(1)}, u32[]{:S(2)}) copy-start(f32[1,2048]{1,0:T(1,128)S(1)} %get-tuple-element.142) | copy-start | bytes 24580
  128.3 228.2 %copy-start.46 = (bf16[2048,128]{0,1:T(8,128)(2,1)}, bf16[2048,128]{0,1:T(8,128)(2,1)S(1)}, u32[]{:S(2)}) copy-start(bf16[2048,128]{0,1:T(8,128)(2,1)S(1)} %all_gather.102) | copy-start | bytes 1572868
  156.5 241.7 %copy-start.151 = (f32[2048]{0:T(1024)}, f32[2048]{0:T(1024)S(1)}, u32[]{:S(2)}) copy-start(f32[2048]{0:T(1024)S(1)} %get-tuple-element.145) | copy-start | bytes 24580
  328.4 327.5 %copy-start.12 = (bf16[512,1536]{1,0:T(8,128)(2,1)}, bf16[512,1536]{1,0:T(8,128)(2,1)S(1)}, u32[]{:S(2)}) copy-start(bf16[512,1536]{1,0:T(8,128)(2,1)S(1)} %fusion.33) | copy-start | bytes 4718596
  497.8 41.8 %copy-start.62 = (f32[32,2048]{1,0:T(8,128)}, f32[32,2048]{1,0:T(8,128)S(1)}, u32[]{:S(2)}) copy-start(f32[32,2048]{1,0:T(8,128)S(1)} %slice.342) | copy-start | bytes 786436
  501.5 33.2 %copy-start.76 = (f32[64,2048]{1,0:T(8,128)S(1)}, f32[64,2048]{1,0:T(8,128)}, u32[]{:S(2)}) copy-start(f32[64,2048]{1,0:T(8,128)} %get-tuple-element.95) | copy-start | bytes 1572868
  502.6 47.3 %copy-start.111 = (f32[16,2048]{1,0:T(8,128)}, f32[16,2048]{1,0:T(8,128)S(1)}, u32[]{:S(2)}) copy-start(f32[16,2048]{1,0:T(8,128)S(1)} %slice.349) | copy-start | bytes 393220
  505.2 44.6 %copy-start.88 = (f32[16,2048]{1,0:T(8,128)}, f32[16,2048]{1,0:T(8,128)S(1)}, u32[]{:S(2)}) copy-start(f32[16,2048]{1,0:T(8,128)S(1)} %slice.348) | copy-start | bytes 393220
  506.3 43.6 %copy-start.113 = (f32[16,2048]{1,0:T(8,128)}, f32[16,2048]{1,0:T(8,128)S(1)}, u32[]{:S(2)}) copy-start(f32[16,2048]{1,0:T(8,128)S(1)} %slice.352) | copy-start | bytes 393220
  507.3 24.9 copy-start.130
  508.0 47.4 %copy-start.126 = (f32[8,2048]{1,0:T(8,128)}, f32[8,2048]{1,0:T(8,128)S(1)}, u32[]{:S(2)}) copy-start(f32[8,2048]{1,0:T(8,128)S(1)} %slice.354) | copy-start | bytes 196612
  508.1 24.1 copy-start.132
  521.7 33.7 %copy-start.162 = (f32[1,2048]{1,0:T(1,128)}, f32[1,2048]{1,0:T(1,128)S(1)}, u32[]{:S(2)}) copy-start(f32[1,2048]{1,0:T(1,128)S(1)} %get-tuple-element.138) | copy-start | bytes 24580
  528.2 50.0 %copy-start.128 = (f32[7,2048]{1,0:T(8,128)}, f32[7,2048]{1,0:T(8,128)S(1)}, u32[]{:S(2)}) copy-start(f32[7,2048]{1,0:T(8,128)S(1)} %slice.353) | copy-start | bytes 172036
  530.5 48.5 %copy-start.109 = (f32[15,2048]{1,0:T(8,128)}, f32[15,2048]{1,0:T(8,128)S(1)}, u32[]{:S(2)}) copy-start(f32[15,2048]{1,0:T(8,128)S(1)} %slice.347) | copy-start | bytes 368644
  534.8 45.7 %copy-start.77 = (f32[31,2048]{1,0:T(8,128)}, f32[31,2048]{1,0:T(8,128)S(1)}, u32[]{:S(2)}) copy-start(f32[31,2048]{1,0:T(8,128)S(1)} %slice.341) | copy-start | bytes 761860
  556.3 21.9 copy-start.190
  677.1 519.7 %copy-start.14 = (bf16[512,1536]{1,0:T(8,128)(2,1)}, bf16[512,1536]{1,0:T(8,128)(2,1)S(1)}, u32[]{:S(2)}) copy-start(bf16[512,1536]{1,0:T(8,128)(2,1)S(1)} %multiply_convert_fusion.3) | copy-start | bytes 4718596
  677.7 549.2 %copy-start.92 = (bf16[512,128]{1,0:T(8,128)(2,1)}, bf16[512,128]{1,0:T(8,128)(2,1)S(1)}, u32[]{:S(2)}) copy-start(bf16[512,128]{1,0:T(8,128)(2,1)S(1)} %fusion.49) | copy-start | bytes 393220
  678.3 579.7 %copy-start.94 = (bf16[512,128]{1,0:T(8,128)(2,1)}, bf16[512,128]{1,0:T(8,128)(2,1)S(1)}, u32[]{:S(2)}) copy-start(bf16[512,128]{1,0:T(8,128)(2,1)S(1)} %fusion.48) | copy-start | bytes 393220
  720.0 812.8 %copy-start.155 = (bf16[512,128]{1,0:T(8,128)(2,1)}, bf16[512,128]{1,0:T(8,128)(2,1)S(1)}, u32[]{:S(2)}) copy-start(bf16[512,128]{1,0:T(8,128)(2,1)S(1)} %fusion.50) | copy-start | bytes 393220
  1235.9 266.7 %copy-start.42 = (bf16[512,1536]{1,0:T(8,128)(2,1)S(1)}, bf16[512,1536]{1,0:T(8,128)(2,1)}, u32[]{:S(2)}) copy-start(bf16[512,1536]{1,0:T(8,128)(2,1)} %gather_fusion.2) | copy-start | bytes 4718596
  1550.1 25.8 copy-start.25
  1722.8 22.1 copy-start.60
  1727.5 22.2 slice-start.7
  1975.4 794.9 %all-gather.45.cloned.1.call-start = ((), (), s32[]{:S(2)}) async-start(), calls=%async_computation.12 | async-start | bytes 15728640 | tf_op jit(solution)/shard_map/all_gather | solution.py:306
  1992.8 996.1 %all-gather.49.cloned.1.call-start = ((), (), s32[]{:S(2)}) async-start(), calls=%async_computation.14 | async-start | bytes 15728640 | tf_op jit(solution)/shard_map/all_gather | solution.py:307
  (177 other events, 1174.7 us)
Sparse Core Ops, SparseCore 0:
  9.6 143.8 all-gather.20
  155.0 150.7 all-gather.22
  307.4 26.5 all-gather.24
  335.4 27.4 all-gather.26
  364.3 114.8 all-gather.28
  480.6 113.5 all-gather.30
  595.7 113.5 all-gather.46
  710.9 242.1 all-gather.36
  954.7 242.1 all-gather.32
  1198.2 28.6 all-gather.38
  1228.5 29.5 all-gather.34
  1259.5 243.0 all-gather.40
  1504.1 28.6 all-gather.42
  1975.5 572.2 all-reduce.95
  2550.8 219.4 all-gather.44
  2772.4 216.3 all-gather.48
where the time goes:
time: 3020 us; the launch traced here: 3010 us
  waiting for transfers between devices  1740 us (58%)
  local copies, waits for them, and re-layouts  543 us (18%)
  blocking collectives  294 us (10%)
  matrix products  234 us (8%)
  other arithmetic  177 us (6%)
    psum x1, waiting for transfers between devices, local(): lax.psum((grad_down_branch, grad_up_branch, grad_down_gelu, grad_up_gelu,...  528 us
    pad x70, local copies, waits for them, and re-layouts, recurrence(): unused, state = lax.associative_scan(combine, (carried, driven), axis=0)  244 us
    all_gather x1, waiting for transfers between devices, local(): lax.all_gather(feed_down, 'shard', axis=0, tiled=True)  234 us
    all_gather x1, waiting for transfers between devices, local(): lax.all_gather(feed_up, 'shard', axis=1, tiled=True)  233 us
    all_gather x1, waiting for transfers between devices, local(): lax.all_gather(feed_gate, 'shard', axis=1, tiled=True)  231 us
    all_gather x1, waiting for transfers between devices, local(): lax.all_gather(grad_work, 'shard', axis=0, tiled=True)  210 us
    all_gather x1, waiting for transfers between devices, local(): lax.all_gather(work_out, 'shard', axis=0, tiled=True)  207 us
    slice x69, local copies, waits for them, and re-layouts, recurrence(): unused, state = lax.associative_scan(combine, (carried, driven), axis=0)  178 us
  transfers between devices with their start and end apart: 16, of which 11 were waited for; matrix products, arithmetic and copies ran while one was open for 16% of the time, Pallas kernels for 0%

commit v1 on v0

--- a/solution.py
+++ b/solution.py
@@ -316,23 +316,26 @@
     grad_tokens = jnp.take(collected[1], my_rows, axis=0)
     part_width = grad_down_branch.shape[1] // shards
     summed = lax.psum(
-        (
-            grad_down_branch,
-            grad_up_branch,
-            grad_down_gelu,
-            grad_up_gelu,
-            grad_down_gates,
-            grad_up_gates,
-            grad_down_merge,
-            grad_up_merge,
-            grad_down_fgate,
-            grad_up_fgate,
-            grad_down_fup,
-            grad_up_fup,
-            grad_down_fdown,
-            grad_up_fdown,
+        lax.psum(
+            (
+                grad_down_branch,
+                grad_up_branch,
+                grad_down_gelu,
+                grad_up_gelu,
+                grad_down_gates,
+                grad_up_gates,
+                grad_down_merge,
+                grad_up_merge,
+                grad_down_fgate,
+                grad_up_fgate,
+                grad_down_fup,
+                grad_up_fup,
+                grad_down_fdown,
+                grad_up_fdown,
+            ),
+            "shard",
         ),
-        ("rep", "shard"),
+        "rep",
     )
     owned = tuple(
         (

time: 3020 us -> 3310 us (1.096)
  waiting for transfers between devices: 1740 us -> 2030 us
    psum x0 -> x1, waiting for transfers between devices: none -> 229 us  [local(): lax.psum(lax.psum((grad_down_branch, grad_up_branch, grad_down_gelu, grad...]
    psum x1, waiting for transfers between devices: 528 us -> 581 us  [local(): lax.psum((grad_down_branch, grad_up_branch, grad_down_gelu, grad_up_gelu,...]
  transfers between devices with their start and end apart: 16 -> 17, of which waited for: 11 -> 12; matrix products, arithmetic and copies ran while one was open for 16% -> 15% of each run, Pallas kernels for 0% -> 0%
where the time goes in v1:
time: 3310 us; the launch traced here: 3300 us
  waiting for transfers between devices  2030 us (61%)
  local copies, waits for them, and re-layouts  544 us (16%)
  blocking collectives  295 us (9%)
  matrix products  234 us (7%)
  other arithmetic  177 us (5%)
    psum x1, waiting for transfers between devices, local(): lax.psum((grad_down_branch, grad_up_branch, grad_down_gelu, grad_up_gelu,...  581 us
    pad x70, local copies, waits for them, and re-layouts, recurrence(): unused, state = lax.associative_scan(combine, (carried, driven), axis=0)  244 us
    all_gather x1, waiting for transfers between devices, local(): lax.all_gather(feed_down, 'shard', axis=0, tiled=True)  234 us
    all_gather x1, waiting for transfers between devices, local(): lax.all_gather(feed_up, 'shard', axis=1, tiled=True)  233 us
    all_gather x1, waiting for transfers between devices, local(): lax.all_gather(feed_gate, 'shard', axis=1, tiled=True)  231 us
    psum x1, waiting for transfers between devices, local(): lax.psum(lax.psum((grad_down_branch, grad_up_branch, grad_down_gelu, grad...  229 us
    all_gather x1, waiting for transfers between devices, local(): lax.all_gather(grad_work, 'shard', axis=0, tiled=True)  210 us
    all_gather x1, waiting for transfers between devices, local(): lax.all_gather(work_out, 'shard', axis=0, tiled=True)  210 us
  transfers between devices with their start and end apart: 17, of which 12 were waited for; matrix products, arithmetic and copies ran while one was open for 15% of the time, Pallas kernels for 0%

profile of v1, /device:TPU:0, one launch (start us, length us, event | category | flops | bytes accessed | tf_op | source)
XLA Modules:
  0.0 3295.3 jit_solution(15167056796754497916)
XLA Ops:
  19.0 15.8 all-gather.1
  35.1 17.6 all_gather.98
  52.7 23.2 all_gather.99
  76.7 16.9 all_gather.95
  93.7 14.5 all-gather
  108.3 20.1 all_gather.102
  128.4 17.1 all-gather.2
  145.5 11.9 all-gather.3
  158.1 21.5 all_gather.106
  179.5 21.5 all_gather.107
  201.0 22.2 all_gather.109
  223.2 22.3 all_gather.110
  245.5 11.9 all-gather.4
  258.0 21.2 all_gather.116
  279.2 22.0 all_gather.113
  301.2 15.2 all_gather.120
  348.1 9.0 copy.113
  362.8 8.3 add_add_fusion
  371.0 9.3 copy.142
  398.1 11.7 exponential_select_fusion
  409.8 9.8 slice.325
  419.6 9.8 slice.326
  429.4 9.8 slice.324
  439.2 9.8 slice.328
  556.3 10.1 slice.323
  566.4 10.1 slice.388
  598.7 8.7 pad.364
  616.2 16.5 pad.367
  638.7 16.5 pad.366
  678.3 30.9 all-gather.47.cloned.1.call-done
  719.9 233.1 %all-gather.37.cloned.1.call-done = bf16[1536,4608]{1,0:T(8,128)(2,1)} async-done(((bf16[1536,1152]{1,0:T(8,128)(2,1)}), bf16[1536,4608]{1,0:T(8,128)(2,1)}) %all-gather.37.cloned.1.call-update) | async-done | bytes 14155792 | tf_op jit(solution)/shard_map/all_gather | solution.py:231
  953.0 12.9 fusion.130
  965.9 230.8 %all-gather.33.cloned.1.call-done = bf16[1536,4608]{1,0:T(8,128)(2,1)} async-done(((bf16[1536,1152]{1,0:T(8,128)(2,1)}), bf16[1536,4608]{1,0:T(8,128)(2,1)}) %all-gather.33.cloned.1.call-update) | async-done | bytes 14155792 | tf_op jit(solution)/shard_map/all_gather | solution.py:230
  1196.7 12.9 fusion.129
  1209.6 17.2 all-gather.39.cloned.1.call-done
  1226.8 9.0 convolution_add_fusion.1
  1235.8 22.2 all-gather.35.cloned.1.call-done
  1258.0 10.0 convolution_add_fusion.2
  1268.0 234.5 %all-gather.41.cloned.1.call-done = bf16[4608,1536]{1,0:T(8,128)(2,1)} async-done(((bf16[1152,1536]{1,0:T(8,128)(2,1)}), bf16[4608,1536]{1,0:T(8,128)(2,1)}) %all-gather.41.cloned.1.call-update) | async-done | bytes 14155792 | tf_op jit(solution)/shard_map/all_gather | solution.py:232
  1502.5 13.3 fusion.95
  1515.8 16.9 all-gather.43.cloned.1.call-done
  1532.7 17.3 multiply_convert_fusion
  1550.0 13.4 fusion.131
  1564.8 10.3 convolution_add_fusion.12
  1598.3 9.8 slice.389
  1615.1 9.8 slice.390
  1714.0 8.7 pad.425
  1727.6 8.6 pad.450
  1736.2 8.8 pad.375
  1749.8 11.2 multiply_add_fusion.1
  1764.0 16.6 pad.426
  1780.6 16.5 pad.427
  1797.1 16.5 pad.451
  1813.6 16.6 pad.452
  1830.2 16.9 pad.370
  1847.1 16.9 pad.428
  1864.0 18.4 multiply_multiply_fusion.5
  1977.1 12.4 convolution_add_fusion.13
  2011.1 581.3 %all-reduce.100.cloned.1.call-done = (f32[1536,128]{0,1:T(8,128)}, f32[128,2048]{1,0:T(8,128)}, f32[1536,128]{0,1:T(8,128)}, f32[128,2048]{1,0:T(8,128)}, f32[20...) async-done(((f32[1536,128]{0,1:T(8,128)}, ...) | async-done | bytes 18087952 | tf_op jit(solution)/shard_map/psum | solution.py:319
  2601.3 209.5 %all-gather.45.cloned.1.call-done = f32[2048,1536]{1,0:T(8,128)} async-done(((f32[512,1536]{1,0:T(8,128)}), f32[2048,1536]{1,0:T(8,128)}) %all-gather.45.cloned.1.call-update) | async-done | bytes 12582928 | tf_op jit(solution)/shard_map/all_gather | solution.py:306
  2810.9 8.3 gather_fusion.1
  2819.1 210.2 %all-gather.49.cloned.1.call-done = f32[2048,1536]{1,0:T(8,128)} async-done(((f32[512,1536]{1,0:T(8,128)}), f32[2048,1536]{1,0:T(8,128)}) %all-gather.49.cloned.1.call-update) | async-done | bytes 12582928 | tf_op jit(solution)/shard_map/all_gather | solution.py:307
  3029.4 9.1 gather_fusion.3
  3043.9 229.5 %all-reduce.98.cloned.1.call-done = (f32[1536,128]{0,1:T(8,128)}, f32[128,2048]{1,0:T(8,128)}, f32[1536,128]{0,1:T(8,128)}, f32[128,2048]{1,0:T(8,128)}, f32[204...) async-done(((f32[1536,128]{0,1:T(8,128)}, ...) | async-done | bytes 18087952 | tf_op jit(solution)/shard_map/psum | solution.py:318
  (800 shorter events, 522.9 us)
Async XLA Ops:
  7.2 311.2 %all-gather.21.cloned.1.call-start = ((), (), s32[]{:S(2)}) async-start(), calls=%async_computation | async-start | bytes 7864320 | tf_op jit(solution)/shard_map/all_gather | solution.py:126
  7.9 321.5 %all-gather.23.cloned.1.call-start = ((), (), s32[]{:S(2)}) async-start(), calls=%async_computation.1 | async-start | bytes 7864320 | tf_op jit(solution)/shard_map/all_gather | solution.py:134
  8.7 332.8 %all-gather.25.cloned.1.call-start = ((), (), s32[]{:S(2)}) async-start(), calls=%async_computation.2 | async-start | bytes 1310720 | tf_op jit(solution)/shard_map/all_gather | solution.py:138
  9.4 353.3 %all-gather.27.cloned.1.call-start = ((), (), s32[]{:S(2)}) async-start(), calls=%async_computation.3 | async-start | bytes 1310720 | tf_op jit(solution)/shard_map/all_gather | solution.py:160
  10.0 645.9 %all-gather.29.cloned.1.call-start = ((), (), s32[]{:S(2)}) async-start(), calls=%async_computation.4 | async-start | bytes 7864320 | tf_op jit(solution)/shard_map/all_gather | solution.py:135
  10.6 657.5 %all-gather.31.cloned.1.call-start = ((), (), s32[]{:S(2)}) async-start(), calls=%async_computation.5 | async-start | bytes 7864320 | tf_op jit(solution)/shard_map/all_gather | solution.py:141
  11.1 698.1 %all-gather.47.cloned.1.call-start = ((), (), s32[]{:S(2)}) async-start(), calls=%async_computation.13 | async-start | bytes 7864320 | tf_op jit(solution)/shard_map/all_gather | solution.py:127
  11.9 941.1 %all-gather.37.cloned.1.call-start = ((), (), s32[]{:S(2)}) async-start(), calls=%async_computation.8 | async-start | bytes 17694720 | tf_op jit(solution)/shard_map/all_gather | solution.py:231
  12.7 22.2 copy-start.211
  12.7 22.4 copy-start.168
  12.7 40.1 %copy-start.157 = (bf16[32,2048]{1,0:T(8,128)(2,1)S(1)}, bf16[32,2048]{1,0:T(8,128)(2,1)}, u32[]{:S(2)}) copy-start(bf16[32,2048]{1,0:T(8,128)(2,1)} %param.52) | copy-start | bytes 393220
  12.7 64.0 %copy-start.204 = (bf16[4,512]{1,0:T(4,128)(2,1)S(1)}, bf16[4,512]{1,0:T(4,128)(2,1)}, u32[]{:S(2)}) copy-start(bf16[4,512]{1,0:T(4,128)(2,1)} %param.41) | copy-start | bytes 12292
  12.7 81.0 %copy-start.206 = (bf16[512]{0:T(512)(128)(2,1)S(1)}, bf16[512]{0:T(512)(128)(2,1)}, u32[]{:S(2)}) copy-start(bf16[512]{0:T(512)(128)(2,1)} %param.42) | copy-start | bytes 3076
  12.7 1184.0 %all-gather.33.cloned.1.call-start = ((), (), s32[]{:S(2)}) async-start(), calls=%async_computation.6 | async-start | bytes 17694720 | tf_op jit(solution)/shard_map/all_gather | solution.py:230
  13.4 94.8 %copy-start.158 = (bf16[2048,32]{0,1:T(8,128)(2,1)S(1)}, bf16[2048,32]{0,1:T(8,128)(2,1)}, u32[]{:S(2)}) copy-start(bf16[2048,32]{0,1:T(8,128)(2,1)} %param.55) | copy-start | bytes 393220
  13.5 114.9 %copy-start.205 = (bf16[4,256]{1,0:T(4,128)(2,1)S(1)}, bf16[4,256]{1,0:T(4,128)(2,1)}, u32[]{:S(2)}) copy-start(bf16[4,256]{1,0:T(4,128)(2,1)} %param.44) | copy-start | bytes 6148
  13.5 132.0 %copy-start.207 = (bf16[512]{0:T(512)(128)(2,1)S(1)}, bf16[512]{0:T(512)(128)(2,1)}, u32[]{:S(2)}) copy-start(bf16[512]{0:T(512)(128)(2,1)} %param.45) | copy-start | bytes 3076
  13.5 144.6 %copy-start.169 = (bf16[1536,32]{0,1:T(8,128)(2,1)S(1)}, bf16[1536,32]{0,1:T(8,128)(2,1)}, u32[]{:S(2)}) copy-start(bf16[1536,32]{0,1:T(8,128)(2,1)} %param.53) | copy-start | bytes 294916
  13.5 166.0 %copy-start.159 = (bf16[32,2048]{1,0:T(8,128)(2,1)S(1)}, bf16[32,2048]{1,0:T(8,128)(2,1)}, u32[]{:S(2)}) copy-start(bf16[32,2048]{1,0:T(8,128)(2,1)} %param.54) | copy-start | bytes 393220
  13.5 1213.3 %all-gather.39.cloned.1.call-start = ((), (), s32[]{:S(2)}) async-start(), calls=%async_computation.9 | async-start | bytes 1474560 | tf_op jit(solution)/shard_map/all_gather | solution.py:166
  14.1 186.9 %copy-start.160 = (bf16[2048,32]{0,1:T(8,128)(2,1)S(1)}, bf16[2048,32]{0,1:T(8,128)(2,1)}, u32[]{:S(2)}) copy-start(bf16[2048,32]{0,1:T(8,128)(2,1)} %param.57) | copy-start | bytes 393220
  14.1 1243.9 %all-gather.35.cloned.1.call-start = ((), (), s32[]{:S(2)}) async-start(), calls=%async_computation.7 | async-start | bytes 1474560 | tf_op jit(solution)/shard_map/all_gather | solution.py:164
  14.8 208.4 %copy-start.170 = (bf16[32,1536]{1,0:T(8,128)(2,1)S(1)}, bf16[32,1536]{1,0:T(8,128)(2,1)}, u32[]{:S(2)}) copy-start(bf16[32,1536]{1,0:T(8,128)(2,1)} %param.58) | copy-start | bytes 294916
  14.8 230.7 %copy-start.209 = (bf16[384]{0:T(512)(128)(2,1)S(1)}, bf16[384]{0:T(512)(128)(2,1)}, u32[]{:S(2)}) copy-start(bf16[384]{0:T(512)(128)(2,1)} %param.47) | copy-start | bytes 2308
  14.9 243.2 %copy-start.171 = (bf16[1536,32]{0,1:T(8,128)(2,1)S(1)}, bf16[1536,32]{0,1:T(8,128)(2,1)}, u32[]{:S(2)}) copy-start(bf16[1536,32]{0,1:T(8,128)(2,1)} %param.61) | copy-start | bytes 294916
  14.9 264.4 %copy-start.172 = (bf16[1536,32]{0,1:T(8,128)(2,1)S(1)}, bf16[1536,32]{0,1:T(8,128)(2,1)}, u32[]{:S(2)}) copy-start(bf16[1536,32]{0,1:T(8,128)(2,1)} %param.59) | copy-start | bytes 294916
  14.9 286.4 %copy-start.173 = (bf16[32,1536]{1,0:T(8,128)(2,1)S(1)}, bf16[32,1536]{1,0:T(8,128)(2,1)}, u32[]{:S(2)}) copy-start(bf16[32,1536]{1,0:T(8,128)(2,1)} %param.64) | copy-start | bytes 294916
  14.9 1487.6 %all-gather.41.cloned.1.call-start = ((), (), s32[]{:S(2)}) async-start(), calls=%async_computation.10 | async-start | bytes 17694720 | tf_op jit(solution)/shard_map/all_gather | solution.py:232
  15.5 1517.2 %all-gather.43.cloned.1.call-start = ((), (), s32[]{:S(2)}) async-start(), calls=%async_computation.11 | async-start | bytes 1474560 | tf_op jit(solution)/shard_map/all_gather | solution.py:167
  16.2 2576.2 %all-reduce.100.cloned.1.call-start = ((), (), s32[]{:S(2)}) async-start(), calls=%async_computation.16 | async-start | bytes 36175872 | tf_op jit(solution)/shard_map/psum | solution.py:319
  34.8 292.0 %copy-start.177 = (f32[1536]{0:T(1024)}, f32[1536]{0:T(1024)S(1)}, u32[]{:S(2)}) copy-start(f32[1536]{0:T(1024)S(1)} %reshape.246) | copy-start | bytes 18436
  52.7 276.1 %copy-start.72 = (bf16[1536,128]{0,1:T(8,128)(2,1)}, bf16[1536,128]{0,1:T(8,128)(2,1)S(1)}, u32[]{:S(2)}) copy-start(bf16[1536,128]{0,1:T(8,128)(2,1)S(1)} %all_gather.98) | copy-start | bytes 1179652
  75.9 259.1 %copy-start.49 = (bf16[128,2048]{1,0:T(8,128)(2,1)}, bf16[128,2048]{1,0:T(8,128)(2,1)S(1)}, u32[]{:S(2)}) copy-start(bf16[128,2048]{1,0:T(8,128)(2,1)S(1)} %all_gather.99) | copy-start | bytes 1572868
  76.7 321.4 %copy-start.198 = (pred[512]{0:T(512)(128)(4,1)}, pred[512]{0:T(512)(128)(4,1)S(1)}, u32[]{:S(2)}) copy-start(pred[512]{0:T(512)(128)(4,1)S(1)} %get-tuple-element.160) | copy-start | bytes 1540
  93.7 242.1 %copy-start.175 = (f32[1,2048]{1,0:T(1,128)}, f32[1,2048]{1,0:T(1,128)S(1)}, u32[]{:S(2)}) copy-start(f32[1,2048]{1,0:T(1,128)S(1)} %get-tuple-element.154) | copy-start | bytes 24580
  93.7 242.1 %copy-start.179 = (f32[1,2048]{1,0:T(1,128)}, f32[1,2048]{1,0:T(1,128)S(1)}, u32[]{:S(2)}) copy-start(f32[1,2048]{1,0:T(1,128)S(1)} %get-tuple-element.155) | copy-start | bytes 24580
  93.7 242.1 %copy-start.181 = (f32[1,2048]{1,0:T(1,128)}, f32[1,2048]{1,0:T(1,128)S(1)}, u32[]{:S(2)}) copy-start(f32[1,2048]{1,0:T(1,128)S(1)} %get-tuple-element.157) | copy-start | bytes 24580
  93.7 242.1 %copy-start.183 = (f32[1,2048]{1,0:T(1,128)}, f32[1,2048]{1,0:T(1,128)S(1)}, u32[]{:S(2)}) copy-start(f32[1,2048]{1,0:T(1,128)S(1)} %get-tuple-element.156) | copy-start | bytes 24580
  128.4 228.7 %copy-start.46 = (bf16[2048,128]{0,1:T(8,128)(2,1)}, bf16[2048,128]{0,1:T(8,128)(2,1)S(1)}, u32[]{:S(2)}) copy-start(bf16[2048,128]{0,1:T(8,128)(2,1)S(1)} %all_gather.102) | copy-start | bytes 1572868
  158.1 240.0 %copy-start.151 = (f32[2048]{0:T(1024)}, f32[2048]{0:T(1024)S(1)}, u32[]{:S(2)}) copy-start(f32[2048]{0:T(1024)S(1)} %get-tuple-element.159) | copy-start | bytes 24580
  328.8 327.0 %copy-start.12 = (bf16[512,1536]{1,0:T(8,128)(2,1)}, bf16[512,1536]{1,0:T(8,128)(2,1)S(1)}, u32[]{:S(2)}) copy-start(bf16[512,1536]{1,0:T(8,128)(2,1)S(1)} %fusion.33) | copy-start | bytes 4718596
  497.7 41.7 %copy-start.62 = (f32[32,2048]{1,0:T(8,128)}, f32[32,2048]{1,0:T(8,128)S(1)}, u32[]{:S(2)}) copy-start(f32[32,2048]{1,0:T(8,128)S(1)} %slice.342) | copy-start | bytes 786436
  501.5 33.2 %copy-start.76 = (f32[64,2048]{1,0:T(8,128)S(1)}, f32[64,2048]{1,0:T(8,128)}, u32[]{:S(2)}) copy-start(f32[64,2048]{1,0:T(8,128)} %get-tuple-element.109) | copy-start | bytes 1572868
  502.5 47.2 %copy-start.111 = (f32[16,2048]{1,0:T(8,128)}, f32[16,2048]{1,0:T(8,128)S(1)}, u32[]{:S(2)}) copy-start(f32[16,2048]{1,0:T(8,128)S(1)} %slice.349) | copy-start | bytes 393220
  505.2 44.6 %copy-start.88 = (f32[16,2048]{1,0:T(8,128)}, f32[16,2048]{1,0:T(8,128)S(1)}, u32[]{:S(2)}) copy-start(f32[16,2048]{1,0:T(8,128)S(1)} %slice.348) | copy-start | bytes 393220
  506.2 43.5 %copy-start.113 = (f32[16,2048]{1,0:T(8,128)}, f32[16,2048]{1,0:T(8,128)S(1)}, u32[]{:S(2)}) copy-start(f32[16,2048]{1,0:T(8,128)S(1)} %slice.352) | copy-start | bytes 393220
  507.3 24.8 copy-start.130
  508.0 47.4 %copy-start.126 = (f32[8,2048]{1,0:T(8,128)}, f32[8,2048]{1,0:T(8,128)S(1)}, u32[]{:S(2)}) copy-start(f32[8,2048]{1,0:T(8,128)S(1)} %slice.354) | copy-start | bytes 196612
  508.0 24.1 copy-start.132
  521.6 33.7 %copy-start.162 = (f32[1,2048]{1,0:T(1,128)}, f32[1,2048]{1,0:T(1,128)S(1)}, u32[]{:S(2)}) copy-start(f32[1,2048]{1,0:T(1,128)S(1)} %get-tuple-element.152) | copy-start | bytes 24580
  528.1 50.0 %copy-start.128 = (f32[7,2048]{1,0:T(8,128)}, f32[7,2048]{1,0:T(8,128)S(1)}, u32[]{:S(2)}) copy-start(f32[7,2048]{1,0:T(8,128)S(1)} %slice.353) | copy-start | bytes 172036
  530.4 48.5 %copy-start.109 = (f32[15,2048]{1,0:T(8,128)}, f32[15,2048]{1,0:T(8,128)S(1)}, u32[]{:S(2)}) copy-start(f32[15,2048]{1,0:T(8,128)S(1)} %slice.347) | copy-start | bytes 368644
  534.7 45.7 %copy-start.77 = (f32[31,2048]{1,0:T(8,128)}, f32[31,2048]{1,0:T(8,128)S(1)}, u32[]{:S(2)}) copy-start(f32[31,2048]{1,0:T(8,128)S(1)} %slice.341) | copy-start | bytes 761860
  677.1 519.6 %copy-start.14 = (bf16[512,1536]{1,0:T(8,128)(2,1)}, bf16[512,1536]{1,0:T(8,128)(2,1)S(1)}, u32[]{:S(2)}) copy-start(bf16[512,1536]{1,0:T(8,128)(2,1)S(1)} %multiply_convert_fusion.3) | copy-start | bytes 4718596
  677.7 549.1 %copy-start.92 = (bf16[512,128]{1,0:T(8,128)(2,1)}, bf16[512,128]{1,0:T(8,128)(2,1)S(1)}, u32[]{:S(2)}) copy-start(bf16[512,128]{1,0:T(8,128)(2,1)S(1)} %fusion.49) | copy-start | bytes 393220
  678.3 579.7 %copy-start.94 = (bf16[512,128]{1,0:T(8,128)(2,1)}, bf16[512,128]{1,0:T(8,128)(2,1)S(1)}, u32[]{:S(2)}) copy-start(bf16[512,128]{1,0:T(8,128)(2,1)S(1)} %fusion.48) | copy-start | bytes 393220
  719.9 812.8 %copy-start.155 = (bf16[512,128]{1,0:T(8,128)(2,1)}, bf16[512,128]{1,0:T(8,128)(2,1)S(1)}, u32[]{:S(2)}) copy-start(bf16[512,128]{1,0:T(8,128)(2,1)S(1)} %fusion.50) | copy-start | bytes 393220
  1235.8 266.7 %copy-start.42 = (bf16[512,1536]{1,0:T(8,128)(2,1)S(1)}, bf16[512,1536]{1,0:T(8,128)(2,1)}, u32[]{:S(2)}) copy-start(bf16[512,1536]{1,0:T(8,128)(2,1)} %gather_fusion.2) | copy-start | bytes 4718596
  1550.0 25.8 copy-start.25
  1722.8 22.2 copy-start.60
  1727.6 22.3 slice-start.7
  1975.2 835.6 %all-gather.45.cloned.1.call-start = ((), (), s32[]{:S(2)}) async-start(), calls=%async_computation.12 | async-start | bytes 15728640 | tf_op jit(solution)/shard_map/all_gather | solution.py:306
  1992.6 1036.8 %all-gather.49.cloned.1.call-start = ((), (), s32[]{:S(2)}) async-start(), calls=%async_computation.14 | async-start | bytes 15728640 | tf_op jit(solution)/shard_map/all_gather | solution.py:307
  2011.1 1262.2 %all-reduce.98.cloned.1.call-start = ((), (), s32[]{:S(2)}) async-start(), calls=%async_computation.15 | async-start | bytes 36175872 | tf_op jit(solution)/shard_map/psum | solution.py:318
  (178 other events, 1192.4 us)
Sparse Core Ops, SparseCore 0:
  9.6 143.6 all-gather.20
  154.8 151.5 all-gather.22
  308.0 25.8 all-gather.24
  335.3 27.4 all-gather.26
  364.2 114.8 all-gather.28
  480.5 113.5 all-gather.30
  595.6 113.5 all-gather.46
  710.8 242.1 all-gather.36
  954.6 242.1 all-gather.32
  1198.1 28.6 all-gather.38
  1228.4 29.5 all-gather.34
  1259.4 243.0 all-gather.40
  1504.0 28.6 all-gather.42
  1975.3 617.0 all-reduce.99
  2594.0 216.8 all-gather.44
  2812.9 216.3 all-gather.48
  3036.8 236.5 all-reduce.97
